TPU v7x, 32 devices: a whole 2x2x4 slice. The times are simulated.
32 devices in a mesh: blk: 2 (over core), inner: 4 (over z), outer: 4 (over y, x).
Axes of the slice: x: 2, y: 2, z: 4, core: 2. Of those that a mesh axis runs over, the one named last changes fastest.
Arguments:
- hidden: bfloat16 [64, 256, 1152], P(('inner', 'outer'), 'blk'), may hold values from -6 to 6
- labels: int32 [64], P(('inner', 'outer')), may hold values from 0 to 1000
- steps_t: int32 [64], P(('inner', 'outer')), may hold values from 0 to 999
- live_slots: int32 [64], P(('inner', 'outer')), may hold values from 0 to 1, as said below
- label_table: bfloat16 [1001, 1152], replicated, may hold values from -6 to 6
- targets: bfloat16 [64, 256, 768], P(('inner', 'outer'), 'blk'), may hold values from -6 to 6
- cotangent: bfloat16 [64, 256, 1152], P(('inner', 'outer'), 'blk'), may hold values from -6 to 6
- weights: float32 [32014336], P(('inner', 'outer'))
- weight_momentum: float32 [32014336], P(('inner', 'outer')), may hold values from -320 to 320
- weight_average: float32 [32014336], P(('inner', 'outer'))
- biases: float32 [20992], P(('inner', 'outer')), may hold values from -1.25 to 1.25
- bias_momentum: float32 [20992], P(('inner', 'outer')), may hold values from -320 to 320
- bias_average: float32 [20992], P(('inner', 'outer')), may hold values from -1.25 to 1.25
Outputs:
- block_out: bfloat16 [64, 256, 1152], P(('inner', 'outer'), 'blk')
- grad_hidden: float32 [64, 256, 1152], P(('inner', 'outer'), 'blk')
- grad_cond: float32 [64, 1152], P(('inner', 'outer'))
- new_weight_momentum: float32 [32014336], P(('inner', 'outer'))
- new_weights: float32 [32014336], P(('inner', 'outer'))
- new_weights_low: bfloat16 [32014336], P(('inner', 'outer'))
- new_weight_average: float32 [32014336], P(('inner', 'outer'))
- new_bias_momentum: float32 [20992], P(('inner', 'outer'))
- new_biases: float32 [20992], P(('inner', 'outer'))
- new_biases_low: bfloat16 [20992], P(('inner', 'outer'))
- new_bias_average: float32 [20992], P(('inner', 'outer'))
Inputs may be any that keep to these rules, and one draw needn't show every extreme that they name: `live_slots`: of the 4 slots that one index of inner and outer holds at least one is live, and in the last such index all are.
All inputs are finite; a program needn't handle non-finite values.
Results may differ from a plain program's by a relative error of at most 0.02.
The roundings to bfloat16 on the way count: a program that leaves them out, or rounds other values in their place, can miss the bound.
Values may be sent and summed in bfloat16 or wider, within the bound.
No kernel may reach another device: no remote copies, remote signals or barrier semaphores. Data moves between devices by JAX's collectives and lax.ppermute only.
A program may use at most 384 MiB of HBM per device.

v0:
```python
import math
import jax
import jax.numpy as jnp
from jax import lax
from jax.sharding import PartitionSpec as P

E = 72
D = 1152
FF = 4608
PH = 2048
ZD = 768
LAMBDA_REPA = 0.5
MOMENTUM = 0.5
AVERAGE = 0.5
LR_COEF = 0.04
BIAS_FACTOR = 4.0
EPS_NORM = 1e-06


def passed_along(block, axis, distance):
    devices = range(lax.axis_size(axis))
    route = [((i - distance) % len(devices), i) for i in devices]
    return lax.ppermute(block, axis, route)


def mat_shapes():
    return [(D, 3 * D), (D, D), (D, FF), (FF, D), (D, 6 * D), (D, PH), (PH, PH), (PH, ZD)]


def bias_shapes():
    return [(D,), (D,), (D,), (FF,), (D,), (6 * D,), (PH,), (PH,), (ZD,)]


def split_shard(flat_vec, shapes, blocks):
    segments = []
    offset = 0
    for shape_now in shapes:
        rows_here = shape_now[0] // blocks
        length = rows_here * math.prod(shape_now[1:])
        segments.append(
            flat_vec[offset : offset + length].reshape((rows_here,) + tuple(shape_now[1:]))
        )
        offset += length
    return segments


def unpack_rows(flat_vec, shapes, blocks):
    line_grid = flat_vec.reshape(blocks, -1)
    segments = []
    offset = 0
    for shape_now in shapes:
        length = shape_now[0] // blocks * math.prod(shape_now[1:])
        segments.append(line_grid[:, offset : offset + length].reshape(shape_now))
        offset += length
    return segments


def outer_grid(segments, n_outer):
    grid_w = jnp.concatenate([segment.reshape(n_outer, -1) for segment in segments[:8]], axis=1)
    return (grid_w, segments[8].reshape(n_outer, -1))


def time_embed(steps_t):
    half_dim = D // 2
    frequency = jnp.exp(-math.log(10000.0) * jnp.arange(half_dim, dtype=jnp.float32) / half_dim)
    angles = steps_t.astype(jnp.float32)[:, None] * frequency[None, :]
    return jnp.concatenate([jnp.cos(angles), jnp.sin(angles)], axis=1)


def modulate(values, scale_v, shift_v):
    center = values - jnp.mean(values, axis=-1, keepdims=True)
    normed = center * lax.rsqrt(jnp.mean(center * center, axis=-1, keepdims=True) + EPS_NORM)
    return normed * (1.0 + scale_v[:, None, :]) + shift_v[:, None, :]


def gelu_tanh(values):
    return jax.nn.gelu(values, approximate=True)


def rms_unit(values):
    return values * lax.rsqrt(jnp.mean(values * values, axis=-1, keepdims=True) + EPS_NORM)


def matmul(left_arr, right_arr):
    return jnp.einsum("...i,ij->...j", left_arr, right_arr, preferred_element_type=jnp.float32)


def matmul_t(left_arr, right_arr):
    return jnp.einsum("...j,ij->...i", left_arr, right_arr, preferred_element_type=jnp.float32)


def outer_sum(left_arr, right_arr):
    return jnp.einsum("sni,snj->ij", left_arr, right_arr, preferred_element_type=jnp.float32)


def column_sum(tensor):
    return jnp.sum(tensor.astype(jnp.float32), axis=(0, 1))


def head_view(tensor):
    return tensor.reshape(tensor.shape[0], tensor.shape[1], -1, E)


def score_block(queries, kv_pair):
    raw_scores = jnp.einsum(
        "snhe,smhe->shnm",
        head_view(queries),
        head_view(kv_pair[..., :D]),
        preferred_element_type=jnp.float32,
    )
    return raw_scores * E ** (-0.5)


def weigh_values(probs_blk, kv_pair):
    mixed_out = jnp.einsum(
        "shnm,smhe->snhe",
        probs_blk.astype(jnp.bfloat16),
        head_view(kv_pair[..., D:]),
        preferred_element_type=jnp.float32,
    )
    return mixed_out.reshape(mixed_out.shape[0], mixed_out.shape[1], D)


def grad_block(queries, kv_pair, log_sum, grad_att):
    probs_blk = jnp.exp(score_block(queries, kv_pair) - log_sum[..., None])
    grad_prob = jnp.einsum(
        "snhe,smhe->shnm",
        head_view(grad_att),
        head_view(kv_pair[..., D:]),
        preferred_element_type=jnp.float32,
    )
    return (probs_blk, grad_prob)


def key_product(grad_scores, kv_pair):
    result = jnp.einsum(
        "shnm,smhe->snhe",
        grad_scores,
        head_view(kv_pair[..., :D]),
        preferred_element_type=jnp.float32,
    )
    return result.reshape(result.shape[0], result.shape[1], D)


def kv_grads(grad_scores, probs_blk, queries, grad_att):
    grad_keys = jnp.einsum(
        "shnm,snhe->smhe", grad_scores, head_view(queries), preferred_element_type=jnp.float32
    ) * E ** (-0.5)
    grad_vals = jnp.einsum(
        "shnm,snhe->smhe",
        probs_blk.astype(jnp.bfloat16),
        head_view(grad_att),
        preferred_element_type=jnp.float32,
    )
    rows_n = grad_keys.shape[1]
    return jnp.concatenate(
        [
            grad_keys.reshape(grad_keys.shape[0], rows_n, D),
            grad_vals.reshape(grad_vals.shape[0], rows_n, D),
        ],
        axis=-1,
    )


def body(
    hidden,
    labels,
    steps_t,
    live_slots,
    label_table,
    targets,
    cotangent,
    weights,
    weight_momentum,
    weight_average,
    biases,
    bias_momentum,
    bias_average,
):
    n_inner = lax.axis_size("inner")
    n_outer = lax.axis_size("outer")
    blocks = n_inner * n_outer
    slots = hidden.shape[0]
    local_tok = hidden.shape[1]
    p_qkv, p_proj, p_up, p_down, p_ada, p_one, p_two, p_three = split_shard(
        weights.astype(jnp.bfloat16), mat_shapes(), blocks
    )
    bias_low = biases.astype(jnp.bfloat16)
    w_qkv, w_proj, w_up, w_down, w_ada, w_one, w_two, w_three, bias_all = (
        lax.all_gather(p_qkv, ("inner", "outer"), axis=0, tiled=True),
        lax.all_gather(p_proj, ("inner", "outer"), axis=0, tiled=True),
        lax.all_gather(p_up, ("inner", "outer"), axis=0, tiled=True),
        lax.all_gather(p_down, ("inner", "outer"), axis=0, tiled=True),
        lax.all_gather(p_ada, ("inner", "outer"), axis=0, tiled=True),
        lax.all_gather(p_one, ("inner", "outer"), axis=0, tiled=True),
        lax.all_gather(p_two, ("inner", "outer"), axis=0, tiled=True),
        lax.all_gather(p_three, ("inner", "outer"), axis=0, tiled=True),
        lax.all_gather(bias_low, ("inner", "outer"), axis=0, tiled=True),
    )
    b_q, b_v, b_proj, b_up, b_down, b_ada, c_one, c_two, c_three = unpack_rows(
        bias_all.astype(jnp.float32), bias_shapes(), blocks
    )
    condition = label_table[labels].astype(jnp.float32) + time_embed(steps_t)
    cond_act, silu_cond = jax.vjp(jax.nn.silu, condition)
    cond_low = cond_act.astype(jnp.bfloat16)
    modulation = matmul(cond_low, w_ada) + b_ada
    shift_a, scale_a, gate_a, shift_m, scale_m, gate_m = [
        modulation[:, part_idx * D : (part_idx + 1) * D] for part_idx in range(6)
    ]
    hidden_f = hidden.astype(jnp.float32)
    mixed_a, pull_a = jax.vjp(modulate, hidden_f, scale_a, shift_a)
    mixed_a_low = mixed_a.astype(jnp.bfloat16)
    qkv_bias = jnp.concatenate([b_q, jnp.zeros((D,), jnp.float32), b_v])
    qkv_low = (matmul(mixed_a_low, w_qkv) + qkv_bias).astype(jnp.bfloat16)
    queries = qkv_low[..., :D]
    near_kv = qkv_low[..., D:]
    far_kv = passed_along(near_kv, "blk", 1)
    near_s = score_block(queries, near_kv)
    far_s = score_block(queries, far_kv)
    row_top = jnp.maximum(jnp.max(near_s, axis=-1), jnp.max(far_s, axis=-1))
    row_total = jnp.sum(jnp.exp(near_s - row_top[..., None]), axis=-1) + jnp.sum(
        jnp.exp(far_s - row_top[..., None]), axis=-1
    )
    log_sum = row_top + jnp.log(row_total)
    attended = weigh_values(jnp.exp(near_s - log_sum[..., None]), near_kv) + weigh_values(
        jnp.exp(far_s - log_sum[..., None]), far_kv
    )
    att_low = attended.astype(jnp.bfloat16)
    branch_a = matmul(att_low, w_proj) + b_proj
    residual = hidden_f + gate_a[:, None, :] * branch_a
    mixed_m, pull_m = jax.vjp(modulate, residual, scale_m, shift_m)
    mixed_m_low = mixed_m.astype(jnp.bfloat16)
    pre_act = matmul(mixed_m_low, w_up) + b_up
    activated, gelu_pull = jax.vjp(gelu_tanh, pre_act)
    act_low = activated.astype(jnp.bfloat16)
    branch_m = matmul(act_low, w_down) + b_down
    output = residual + gate_m[:, None, :] * branch_m
    out_low = output.astype(jnp.bfloat16)
    hid_one = matmul(out_low, w_one) + c_one
    act_one, silu_one = jax.vjp(jax.nn.silu, hid_one)
    one_low = act_one.astype(jnp.bfloat16)
    hid_two = matmul(one_low, w_two) + c_two
    act_two, silu_two = jax.vjp(jax.nn.silu, hid_two)
    two_low = act_two.astype(jnp.bfloat16)
    projection = matmul(two_low, w_three) + c_three
    live_f = live_slots.astype(jnp.float32)[:, None, None]
    unit_proj, unit_pull = jax.vjp(rms_unit, projection)
    grad_proj = unit_pull(-LAMBDA_REPA * live_f * rms_unit(targets.astype(jnp.float32)))[0].astype(
        jnp.bfloat16
    )
    grad_pthree = outer_sum(two_low, grad_proj)
    grad_cthree = column_sum(grad_proj)
    grad_htwo = silu_two(matmul_t(grad_proj, w_three))[0].astype(jnp.bfloat16)
    grad_ptwo = outer_sum(one_low, grad_htwo)
    grad_ctwo = column_sum(grad_htwo)
    grad_hone = silu_one(matmul_t(grad_htwo, w_two))[0].astype(jnp.bfloat16)
    grad_pone = outer_sum(out_low, grad_hone)
    grad_cone = column_sum(grad_hone)
    grad_output = cotangent.astype(jnp.float32) * live_f + matmul_t(grad_hone, w_one)
    grad_gate_m = jnp.sum(grad_output * branch_m, axis=1)
    grad_bm = (gate_m[:, None, :] * grad_output).astype(jnp.bfloat16)
    grad_wdown = outer_sum(act_low, grad_bm)
    grad_bdown = column_sum(grad_bm)
    grad_pre = gelu_pull(matmul_t(grad_bm, w_down))[0].astype(jnp.bfloat16)
    grad_wup = outer_sum(mixed_m_low, grad_pre)
    grad_bup = column_sum(grad_pre)
    grad_res_m, grad_scale_m, grad_shift_m = pull_m(matmul_t(grad_pre, w_up))
    grad_residual = grad_output + grad_res_m
    grad_gate_a = jnp.sum(grad_residual * branch_a, axis=1)
    grad_ba = (gate_a[:, None, :] * grad_residual).astype(jnp.bfloat16)
    grad_wproj = outer_sum(att_low, grad_ba)
    grad_bproj = column_sum(grad_ba)
    grad_att = matmul_t(grad_ba, w_proj).astype(jnp.bfloat16)
    near_p, near_dp = grad_block(queries, near_kv, log_sum, grad_att)
    far_p, far_dp = grad_block(queries, far_kv, log_sum, grad_att)
    row_delta = jnp.sum(near_p * near_dp, axis=-1) + jnp.sum(far_p * far_dp, axis=-1)
    near_ds = (near_p * (near_dp - row_delta[..., None])).astype(jnp.bfloat16)
    far_ds = (far_p * (far_dp - row_delta[..., None])).astype(jnp.bfloat16)
    grad_query = (key_product(near_ds, near_kv) + key_product(far_ds, far_kv)) * E ** (-0.5)
    far_dkv = kv_grads(far_ds, far_p, queries, grad_att)
    home_dkv = passed_along(far_dkv.astype(jnp.bfloat16), "blk", -1).astype(far_dkv.dtype)
    near_dkv = kv_grads(near_ds, near_p, queries, grad_att)
    grad_qkv = jnp.concatenate([grad_query, near_dkv + home_dkv], axis=-1).astype(jnp.bfloat16)
    grad_wqkv = outer_sum(mixed_a_low, grad_qkv)
    qkv_sums = column_sum(grad_qkv)
    grad_hid_a, grad_scale_a, grad_shift_a = pull_a(matmul_t(grad_qkv, w_qkv))
    grad_input = grad_residual + grad_hid_a
    grad_mod_part = jnp.concatenate(
        [grad_shift_a, grad_scale_a, grad_gate_a, grad_shift_m, grad_scale_m, grad_gate_m], axis=1
    )
    grad_mod = lax.psum(grad_mod_part.astype(jnp.bfloat16), "blk")
    grad_wada = 0.5 * jnp.einsum(
        "si,sj->ij", cond_low, grad_mod, preferred_element_type=jnp.float32
    )
    grad_bada = 0.5 * jnp.sum(grad_mod.astype(jnp.float32), axis=0)
    grad_cond = silu_cond(matmul_t(grad_mod, w_ada))[0]
    bias_terms = (
        qkv_sums[:D],
        qkv_sums[2 * D :],
        grad_bproj,
        grad_bup,
        grad_bdown,
        grad_bada,
        grad_cone,
        grad_ctwo,
        grad_cthree,
    )
    bias_grid = jnp.concatenate(
        [segment.reshape(blocks, -1) for segment in bias_terms], axis=1
    ).reshape(-1)
    inner_parts = (
        lax.psum_scatter(
            grad_wqkv.astype(jnp.bfloat16), "inner", scatter_dimension=0, tiled=True
        ).astype(jnp.float32),
        lax.psum_scatter(
            grad_wproj.astype(jnp.bfloat16), "inner", scatter_dimension=0, tiled=True
        ).astype(jnp.float32),
        lax.psum_scatter(
            grad_wup.astype(jnp.bfloat16), "inner", scatter_dimension=0, tiled=True
        ).astype(jnp.float32),
        lax.psum_scatter(
            grad_wdown.astype(jnp.bfloat16), "inner", scatter_dimension=0, tiled=True
        ).astype(jnp.float32),
        lax.psum_scatter(
            grad_wada.astype(jnp.bfloat16), "inner", scatter_dimension=0, tiled=True
        ).astype(jnp.float32),
        lax.psum_scatter(
            grad_pone.astype(jnp.bfloat16), "inner", scatter_dimension=0, tiled=True
        ).astype(jnp.float32),
        lax.psum_scatter(
            grad_ptwo.astype(jnp.bfloat16), "inner", scatter_dimension=0, tiled=True
        ).astype(jnp.float32),
        lax.psum_scatter(
            grad_pthree.astype(jnp.bfloat16), "inner", scatter_dimension=0, tiled=True
        ).astype(jnp.float32),
        lax.psum_scatter(
            bias_grid.astype(jnp.bfloat16), "inner", scatter_dimension=0, tiled=True
        ).astype(jnp.float32),
    )
    grid_w, grid_b = outer_grid(inner_parts, n_outer)
    summed_w, summed_b = (
        lax.psum(grid_w.astype(jnp.bfloat16), ("blk", "outer")).astype(jnp.float32),
        lax.psum(grid_b.astype(jnp.bfloat16), ("blk", "outer")).astype(jnp.float32),
    )
    own_index = lax.axis_index("outer")
    grad_w_flat = lax.dynamic_index_in_dim(summed_w, own_index, 0, keepdims=False)
    grad_b_flat = lax.dynamic_index_in_dim(summed_b, own_index, 0, keepdims=False)
    images_all = slots * blocks
    tokens_img = local_tok * lax.axis_size("blk")
    rate_w = LR_COEF / math.sqrt(images_all * tokens_img)
    rate_b = BIAS_FACTOR * rate_w
    mom_w = MOMENTUM * weight_momentum + grad_w_flat
    new_w = weights - rate_w * (grad_w_flat + MOMENTUM * mom_w)
    avg_w = AVERAGE * weight_average + (1.0 - AVERAGE) * new_w
    mom_b = MOMENTUM * bias_momentum + grad_b_flat
    new_b = biases - rate_b * (grad_b_flat + MOMENTUM * mom_b)
    avg_b = AVERAGE * bias_average + (1.0 - AVERAGE) * new_b
    return (
        out_low,
        grad_input,
        grad_cond,
        mom_w,
        new_w,
        new_w.astype(jnp.bfloat16),
        avg_w,
        mom_b,
        new_b,
        new_b.astype(jnp.bfloat16),
        avg_b,
    )


def solution(mesh):
    in_specs = (
        P(("inner", "outer"), "blk", None),
        P(("inner", "outer")),
        P(("inner", "outer")),
        P(("inner", "outer")),
        P(),
        P(("inner", "outer"), "blk", None),
        P(("inner", "outer"), "blk", None),
        P(("inner", "outer")),
        P(("inner", "outer")),
        P(("inner", "outer")),
        P(("inner", "outer")),
        P(("inner", "outer")),
        P(("inner", "outer")),
    )
    out_specs = (
        P(("inner", "outer"), "blk", None),
        P(("inner", "outer"), "blk", None),
        P(("inner", "outer"), None),
        P(("inner", "outer")),
        P(("inner", "outer")),
        P(("inner", "outer")),
        P(("inner", "outer")),
        P(("inner", "outer")),
        P(("inner", "outer")),
        P(("inner", "outer")),
        P(("inner", "outer")),
    )
    return jax.shard_map(body, mesh=mesh, in_specs=in_specs, out_specs=out_specs, check_vma=False)
```

profile of v0, /device:TPU:0, one launch (start us, length us, event | category | flops | bytes accessed | tf_op | source)
XLA Modules:
  0.0 2376.6 jit_solution(2534763386764745877)
XLA Ops:
  35.4 80.9 %all-reduce = bf16[20992]{0:T(1024)(128)(2,1)} all-reduce(bf16[20992]{0:T(1024)(128)(2,1)S(1)} %dynamic-update-slice), channel_id=1, replica_groups=mesh['blk'=2,'inner'=4,'outer'=4] {'inner','outer'}, use_global_device_ids=true, to_apply=%add | all-reduce | flops 20992 | bytes 83968
  125.7 79.5 %all-gather.9.cloned.1.call-done = bf16[1152,6912]{1,0:T(8,128)(2,1)} async-done(((bf16[72,6912]{1,0:T(8,128)(2,1)}), bf16[1152,6912]{1,0:T(8,128)(2,1)}) %all-gather.9.cloned.1.call-update) | async-done | bytes 15925264 | tf_op jit(solution)/shard_map/all_gather | solution.py:194
  213.0 102.7 %all-gather.11.cloned.1.call-done = bf16[1152,3456]{1,0:T(8,128)(2,1)} async-done(((bf16[72,3456]{1,0:T(8,128)(2,1)}), bf16[1152,3456]{1,0:T(8,128)(2,1)}) %all-gather.11.cloned.1.call-update) | async-done | bytes 7962640 | tf_op jit(solution)/shard_map/all_gather | solution.py:190
  315.7 8.8 add_convert_fusion
  365.8 15.1 all-gather.13.cloned.1.call-done
  388.3 127.6 %all-gather.15.cloned.1.call-done = bf16[1152,4608]{1,0:T(8,128)(2,1)} async-done(((bf16[72,4608]{1,0:T(8,128)(2,1)}), bf16[1152,4608]{1,0:T(8,128)(2,1)}) %all-gather.15.cloned.1.call-update) | async-done | bytes 10616848 | tf_op jit(solution)/shard_map/all_gather | solution.py:192
  516.0 12.2 fusion.9
  528.1 122.7 %all-gather.17.cloned.1.call-done = bf16[4608,1152]{1,0:T(8,128)(2,1)} async-done(((bf16[288,1152]{1,0:T(8,128)(2,1)}), bf16[4608,1152]{1,0:T(8,128)(2,1)}) %all-gather.17.cloned.1.call-update) | async-done | bytes 10616848 | tf_op jit(solution)/shard_map/all_gather | solution.py:193
  650.9 14.5 add_convert_fusion.1
  665.4 66.8 %all-gather.19.cloned.1.call-done = bf16[1152,2048]{1,0:T(8,128)(2,1)} async-done(((bf16[72,2048]{1,0:T(8,128)(2,1)}), bf16[1152,2048]{1,0:T(8,128)(2,1)}) %all-gather.19.cloned.1.call-update) | async-done | bytes 4718608 | tf_op jit(solution)/shard_map/all_gather | solution.py:195
  738.9 107.6 %all-gather.21.cloned.1.call-done = bf16[2048,2048]{1,0:T(8,128)(2,1)} async-done(((bf16[128,2048]{1,0:T(8,128)(2,1)}), bf16[2048,2048]{1,0:T(8,128)(2,1)}) %all-gather.21.cloned.1.call-update) | async-done | bytes 8388624 | tf_op jit(solution)/shard_map/all_gather | solution.py:196
  846.5 11.2 fusion.20
  857.7 57.9 %all-gather.23.cloned.1.call-done = bf16[2048,768]{1,0:T(8,128)(2,1)} async-done(((bf16[128,768]{1,0:T(8,128)(2,1)}), bf16[2048,768]{1,0:T(8,128)(2,1)}) %all-gather.23.cloned.1.call-update) | async-done | bytes 3145744 | tf_op jit(solution)/shard_map/all_gather | solution.py:197
  928.1 9.1 fusion.115
  941.9 17.3 fusion.114
  959.2 12.2 multiply_reduce_fusion.7
  993.5 10.9 bitcast_convert_fusion
  1073.9 11.1 fusion
  1085.1 13.1 fusion.1
  1101.6 8.8 fusion.68
  1132.1 48.8 %reduce-scatter.19.cloned.1.call-done = bf16[288,2048]{1,0:T(8,128)(2,1)} async-done(((bf16[1152,2048]{1,0:T(8,128)(2,1)}), bf16[288,2048]{1,0:T(8,128)(2,1)}) %reduce-scatter.19.cloned.1.call-update) | async-done | bytes 1179664 | tf_op jit(solution)/shard_map/reduce_scatter | solution.py:327
  1184.1 144.1 %reduce-scatter.21.cloned.1.call-done = bf16[512,2048]{1,0:T(8,128)(2,1)} async-done(((bf16[2048,2048]{1,0:T(8,128)(2,1)}), bf16[512,2048]{1,0:T(8,128)(2,1)}) %reduce-scatter.21.cloned.1.call-update) | async-done | bytes 2097168 | tf_op jit(solution)/shard_map/reduce_scatter | solution.py:330
  1331.4 138.6 %reduce-scatter.9.cloned.1.call-done = bf16[288,3456]{1,0:T(8,128)(2,1)} async-done(((bf16[1152,3456]{1,0:T(8,128)(2,1)}), bf16[288,3456]{1,0:T(8,128)(2,1)}) %reduce-scatter.9.cloned.1.call-update) | async-done | bytes 1990672 | tf_op jit(solution)/shard_map/reduce_scatter | solution.py:312
  1477.9 175.2 %reduce-scatter.13.cloned.1.call-done = bf16[288,4608]{1,0:T(8,128)(2,1)} async-done(((bf16[1152,4608]{1,0:T(8,128)(2,1)}), bf16[288,4608]{1,0:T(8,128)(2,1)}) %reduce-scatter.13.cloned.1.call-update) | async-done | bytes 2654224 | tf_op jit(solution)/shard_map/reduce_scatter | solution.py:318
  1662.9 173.6 %reduce-scatter.15.cloned.1.call-done = bf16[1152,1152]{1,0:T(8,128)(2,1)} async-done(((bf16[4608,1152]{1,0:T(8,128)(2,1)}), bf16[1152,1152]{1,0:T(8,128)(2,1)}) %reduce-scatter.15.cloned.1.call-update) | async-done | bytes 2654224 | tf_op jit(solution)/shard_map/reduce_scatter | solution.py:321
  1845.2 262.1 %reduce-scatter.17.cloned.1.call-done = bf16[288,6912]{1,0:T(8,128)(2,1)} async-done(((bf16[1152,6912]{1,0:T(8,128)(2,1)}), bf16[288,6912]{1,0:T(8,128)(2,1)}) %reduce-scatter.17.cloned.1.call-update) | async-done | bytes 3981328 | tf_op jit(solution)/shard_map/reduce_scatter | solution.py:324
  2129.0 18.7 all-reduce.1
  2148.0 29.0 %psum.23 = bf16[4,1312]{1,0:T(4,128)(2,1)S(1)} all-reduce(bf16[4,1312]{1,0:T(4,128)(2,1)S(1)} %convert_element_type.227), channel_id=1, replica_groups=mesh['blk'=2,'inner'=4,'outer'=4] {'blk','outer'}, use_global_device_ids=true, to_apply=%region_42.43 | all-reduce | flops 5248 | bytes 20992 | tf_op jit(solution)/shard_map/psum | solution.py:343
  2178.2 10.7 fusion.92
  2188.9 146.4 %all-reduce.4.cloned.1.call-done = bf16[4,2000896]{1,0:T(4,128)(2,1)} async-done(((bf16[4,2000896]{1,0:T(4,128)(2,1)}), bf16[4,2000896]{1,0:T(4,128)(2,1)}) %all-reduce.4.cloned.1.call-update) | async-done | bytes 16007184 | tf_op jit(solution)/shard_map/psum | solution.py:342
  2335.2 9.6 dynamic-slice_convert_fusion
  2344.8 20.1 add_multiply_fusion
  (371 shorter events, 293.4 us)
Async XLA Ops:
  7.2 116.3 %copy-start = (bf16[1001,1152]{1,0:T(8,128)(2,1)S(1)}, bf16[1001,1152]{1,0:T(8,128)(2,1)}, u32[]{:S(2)}) copy-start(bf16[1001,1152]{1,0:T(8,128)(2,1)} %param.17) | copy-start | bytes 6918916
  7.2 198.0 %all-gather.9.cloned.1.call-start = ((), (), s32[]{:S(2)}) async-start(), calls=%async_computation.8 | async-start | bytes 16920576 | tf_op jit(solution)/shard_map/all_gather | solution.py:194
  16.9 298.7 %all-gather.11.cloned.1.call-start = ((), (), s32[]{:S(2)}) async-start(), calls=%async_computation.9 | async-start | bytes 8460288 | tf_op jit(solution)/shard_map/all_gather | solution.py:190
  18.4 362.5 %all-gather.13.cloned.1.call-start = ((), (), s32[]{:S(2)}) async-start(), calls=%async_computation.10 | async-start | bytes 2820096 | tf_op jit(solution)/shard_map/all_gather | solution.py:191
  19.3 496.6 %all-gather.15.cloned.1.call-start = ((), (), s32[]{:S(2)}) async-start(), calls=%async_computation.11 | async-start | bytes 11280384 | tf_op jit(solution)/shard_map/all_gather | solution.py:192
  24.2 626.7 %all-gather.17.cloned.1.call-start = ((), (), s32[]{:S(2)}) async-start(), calls=%async_computation.12 | async-start | bytes 11280384 | tf_op jit(solution)/shard_map/all_gather | solution.py:193
  25.9 93.5 %copy-start.74 = (s32[4]{0:T(128)S(1)}, s32[4]{0:T(128)}, u32[]{:S(2)}) copy-start(s32[4]{0:T(128)} %param.15) | copy-start | bytes 52
  25.9 98.9 %copy-start.8 = (bf16[4,128,1152]{2,1,0:T(8,128)(2,1)S(1)}, bf16[4,128,1152]{2,1,0:T(8,128)(2,1)}, u32[]{:S(2)}) copy-start(bf16[4,128,1152]{2,1,0:T(8,128)(2,1)} %param.13) | copy-start | bytes 3538948
  25.9 706.3 %all-gather.19.cloned.1.call-start = ((), (), s32[]{:S(2)}) async-start(), calls=%async_computation.13 | async-start | bytes 5013504 | tf_op jit(solution)/shard_map/all_gather | solution.py:195
  29.6 816.9 %all-gather.21.cloned.1.call-start = ((), (), s32[]{:S(2)}) async-start(), calls=%async_computation.14 | async-start | bytes 8912896 | tf_op jit(solution)/shard_map/all_gather | solution.py:196
  33.7 881.9 %all-gather.23.cloned.1.call-start = ((), (), s32[]{:S(2)}) async-start(), calls=%async_computation.15 | async-start | bytes 3342336 | tf_op jit(solution)/shard_map/all_gather | solution.py:197
  119.3 85.9 %copy-start.47 = (f32[6912]{0:T(1024)S(1)}, f32[6912]{0:T(1024)}, u32[]{:S(2)}) copy-start(f32[6912]{0:T(1024)} %add.266) | copy-start | bytes 82948
  124.0 88.9 %copy-start.39 = (bf16[4,1152]{1,0:T(4,128)(2,1)}, bf16[4,1152]{1,0:T(4,128)(2,1)S(1)}, u32[]{:S(2)}) copy-start(bf16[4,1152]{1,0:T(4,128)(2,1)S(1)} %gather_fusion) | copy-start | bytes 27652
  125.0 190.7 %copy-start.48 = (f32[4,128]{1,0:T(4,128)}, f32[4,128]{1,0:T(4,128)S(1)}, u32[]{:S(2)}) copy-start(f32[4,128]{1,0:T(4,128)S(1)} %broadcast_multiply_fusion.1) | copy-start | bytes 6148
  125.5 87.5 %copy-start.57 = (f32[4,128]{1,0:T(4,128)}, f32[4,128]{1,0:T(4,128)S(1)}, u32[]{:S(2)}) copy-start(f32[4,128]{1,0:T(4,128)S(1)} %fusion.67) | copy-start | bytes 6148
  125.5 190.2 %copy-start.55 = (f32[4,128]{1,0:T(4,128)}, f32[4,128]{1,0:T(4,128)S(1)}, u32[]{:S(2)}) copy-start(f32[4,128]{1,0:T(4,128)S(1)} %fusion.94) | copy-start | bytes 6148
  125.7 79.5 %copy-start.43 = (f32[4,576]{1,0:T(4,128)}, f32[4,576]{1,0:T(4,128)S(1)}, u32[]{:S(2)}) copy-start(f32[4,576]{1,0:T(4,128)S(1)} %get-tuple-element.63) | copy-start | bytes 27652
  125.7 79.5 %copy-start.45 = (f32[4,576]{1,0:T(4,128)}, f32[4,576]{1,0:T(4,128)S(1)}, u32[]{:S(2)}) copy-start(f32[4,576]{1,0:T(4,128)S(1)} %get-tuple-element.64) | copy-start | bytes 27652
  213.0 111.5 %copy-start.41 = (f32[4,1152]{1,0:T(4,128)}, f32[4,1152]{1,0:T(4,128)S(1)}, u32[]{:S(2)}) copy-start(f32[4,1152]{1,0:T(4,128)S(1)} %get-tuple-element.51) | copy-start | bytes 55300
  213.0 111.5 %copy-start.61 = (f32[4,1152]{1,0:T(4,128)}, f32[4,1152]{1,0:T(4,128)S(1)}, u32[]{:S(2)}) copy-start(f32[4,1152]{1,0:T(4,128)S(1)} %get-tuple-element.50) | copy-start | bytes 55300
  213.0 303.0 %copy-start.59 = (f32[4,1152]{1,0:T(4,128)}, f32[4,1152]{1,0:T(4,128)S(1)}, u32[]{:S(2)}) copy-start(f32[4,1152]{1,0:T(4,128)S(1)} %get-tuple-element.48) | copy-start | bytes 55300
  327.1 17.0 collective-permute-start
  328.0 799.2 %reduce-scatter.11.cloned.1.call-start = ((), (), s32[]{:S(2)}) async-start(), calls=%async_computation.17 | async-start | bytes 3317760 | tf_op jit(solution)/shard_map/reduce_scatter | solution.py:315
  978.8 150.7 %reduce-scatter.23.cloned.1.call-start = ((), (), s32[]{:S(2)}) async-start(), calls=%async_computation.23 | async-start | bytes 3932160 | tf_op jit(solution)/shard_map/reduce_scatter | solution.py:333
  985.7 195.2 %reduce-scatter.19.cloned.1.call-start = ((), (), s32[]{:S(2)}) async-start(), calls=%async_computation.21 | async-start | bytes 5898240 | tf_op jit(solution)/shard_map/reduce_scatter | solution.py:327
  993.4 334.8 %reduce-scatter.21.cloned.1.call-start = ((), (), s32[]{:S(2)}) async-start(), calls=%async_computation.22 | async-start | bytes 10485760 | tf_op jit(solution)/shard_map/reduce_scatter | solution.py:330
  1004.4 465.6 %reduce-scatter.9.cloned.1.call-start = ((), (), s32[]{:S(2)}) async-start(), calls=%async_computation.16 | async-start | bytes 9953280 | tf_op jit(solution)/shard_map/reduce_scatter | solution.py:312
  1038.4 22.4 collective-permute-start.1
  1073.2 579.8 %reduce-scatter.13.cloned.1.call-start = ((), (), s32[]{:S(2)}) async-start(), calls=%async_computation.18 | async-start | bytes 13271040 | tf_op jit(solution)/shard_map/reduce_scatter | solution.py:318
  1085.0 751.4 %reduce-scatter.15.cloned.1.call-start = ((), (), s32[]{:S(2)}) async-start(), calls=%async_computation.19 | async-start | bytes 13271040 | tf_op jit(solution)/shard_map/reduce_scatter | solution.py:321
  1098.2 1009.1 %reduce-scatter.17.cloned.1.call-start = ((), (), s32[]{:S(2)}) async-start(), calls=%async_computation.20 | async-start | bytes 19906560 | tf_op jit(solution)/shard_map/reduce_scatter | solution.py:324
  1127.1 1208.1 %all-reduce.4.cloned.1.call-start = ((), (), s32[]{:S(2)}) async-start(), calls=%async_computation.24 | async-start | bytes 32014336 | tf_op jit(solution)/shard_map/psum | solution.py:342
  (77 other events, 598.7 us)
Sparse Core Ops, SparseCore 0:
  17.1 188.0 all-gather.8
  208.5 107.1 all-gather.10
  318.4 62.4 all-gather.12
  383.5 132.4 all-gather.14
  519.2 131.6 all-gather.16
  653.5 78.6 all-gather.18
  735.0 111.4 all-gather.20
  849.2 66.3 all-gather.22
  978.9 51.1 reduce-scatter.10
  1032.8 59.9 reduce-scatter.22
  1095.6 85.2 reduce-scatter.18
  1183.1 144.9 reduce-scatter.20
  1331.1 138.7 reduce-scatter.8
  1472.3 180.6 reduce-scatter.12
  1655.2 181.1 reduce-scatter.14
  1838.8 268.4 reduce-scatter.16
  2124.0 211.2 all-reduce.3
where the time goes:
time: 2390 us; the launch traced here: 2380 us
  waiting for transfers between devices  1770 us (74%)
  matrix products  247 us (10%)
  local copies, waits for them, and re-layouts  137 us (6%)
  blocking collectives  133 us (6%)
  other arithmetic  73.7 us (3%)
    reduce_scatter x1, waiting for transfers between devices, body(): lax.psum_scatter(grad_wada.astype(jnp.bfloat16), 'inner', scatter_dimensi...  262 us
    reduce_scatter x1, waiting for transfers between devices, body(): lax.psum_scatter(grad_wup.astype(jnp.bfloat16), 'inner', scatter_dimensio...  175 us
    reduce_scatter x1, waiting for transfers between devices, body(): lax.psum_scatter(grad_wdown.astype(jnp.bfloat16), 'inner', scatter_dimens...  174 us
    psum x1, waiting for transfers between devices, body(): lax.psum(grid_w.astype(jnp.bfloat16), ('blk', 'outer')).astype(jnp.float32)  146 us
    reduce_scatter x1, waiting for transfers between devices, body(): lax.psum_scatter(grad_ptwo.astype(jnp.bfloat16), 'inner', scatter_dimensi...  144 us
    reduce_scatter x1, waiting for transfers between devices, body(): lax.psum_scatter(grad_wqkv.astype(jnp.bfloat16), 'inner', scatter_dimensi...  139 us
    all_gather x1, waiting for transfers between devices, body(): lax.all_gather(p_up, ('inner', 'outer'), axis=0, tiled=True)  128 us
    all_gather x1, waiting for transfers between devices, body(): lax.all_gather(p_down, ('inner', 'outer'), axis=0, tiled=True)  123 us
  transfers between devices with their start and end apart: 19, of which 15 were waited for; matrix products, arithmetic and copies ran while one was open for 13% of the time, Pallas kernels for 0%

commit v1 on v0

--- a/solution.py
+++ b/solution.py
@@ -15,6 +15,22 @@
 LR_COEF = 0.04
 BIAS_FACTOR = 4.0
 EPS_NORM = 1e-06
+
+
+def ring_gather(x, axis, dim):
+    ways, here, hop = (lax.axis_size(axis), lax.axis_index(axis), x.shape[dim])
+    shape = [n * ways if d == dim else n for d, n in enumerate(x.shape)]
+    full = lax.dynamic_update_slice_in_dim(jnp.zeros(shape, x.dtype), x, here * hop, axis=dim)
+    going_up = going_down = x
+    for far in range(1, ways // 2 + 1):
+        going_up = lax.ppermute(going_up, axis, [(d, (d + 1) % ways) for d in range(ways)])
+        full = lax.dynamic_update_slice_in_dim(full, going_up, (here - far) % ways * hop, axis=dim)
+        if 2 * far < ways:
+            going_down = lax.ppermute(going_down, axis, [(d, (d - 1) % ways) for d in range(ways)])
+            full = lax.dynamic_update_slice_in_dim(
+                full, going_down, (here + far) % ways * hop, axis=dim
+            )
+    return full
 
 
 def passed_along(block, axis, distance):
@@ -192,7 +208,7 @@
         lax.all_gather(p_up, ("inner", "outer"), axis=0, tiled=True),
         lax.all_gather(p_down, ("inner", "outer"), axis=0, tiled=True),
         lax.all_gather(p_ada, ("inner", "outer"), axis=0, tiled=True),
-        lax.all_gather(p_one, ("inner", "outer"), axis=0, tiled=True),
+        ring_gather(p_one, ("inner", "outer"), 0),
         lax.all_gather(p_two, ("inner", "outer"), axis=0, tiled=True),
         lax.all_gather(p_three, ("inner", "outer"), axis=0, tiled=True),
         lax.all_gather(bias_low, ("inner", "outer"), axis=0, tiled=True),

time: 2390 us -> 2370 us (level)
  waiting for transfers between devices: 1770 us -> 1690 us
  starting transfers between devices: 0.92 us -> 34.6 us
  local copies, waits for them, and re-layouts: 137 us -> 161 us
    ppermute x0 -> x15, waiting for transfers between devices: none -> 83.2 us  [the longest x8 68.5 us: ring_gather(): lax.ppermute(going_up, axis, [(d, (d + 1) % ways) for d in range(ways)])]
    all_gather x1 -> x0, waiting for transfers between devices: 66.8 us -> none  [body(): lax.all_gather(p_one, ('inner', 'outer'), axis=0, tiled=True)]
    all_gather x1, waiting for transfers between devices: 79.5 us -> 14.4 us  [body(): lax.all_gather(p_ada, ('inner', 'outer'), axis=0, tiled=True)]
    ppermute x0 -> x15, starting transfers between devices: none -> 33.7 us  [the longest x7 21.3 us: ring_gather(): lax.ppermute(going_down, axis, [(d, (d - 1) % ways) for d in range(ways)])]
  transfers between devices with their start and end apart: 19 -> 33, of which waited for: 15 -> 22; matrix products, arithmetic and copies ran while one was open for 13% -> 15% of each run, Pallas kernels for 0% -> 0%
where the time goes in v1:
time: 2370 us; the launch traced here: 2360 us
  waiting for transfers between devices  1690 us (71%)
  matrix products  250 us (11%)
  local copies, waits for them, and re-layouts  161 us (7%)
  blocking collectives  131 us (6%)
  other arithmetic  79.1 us (3%)
  starting transfers between devices  34.6 us (1%)
    reduce_scatter x1, waiting for transfers between devices, body(): lax.psum_scatter(grad_wada.astype(jnp.bfloat16), 'inner', scatter_dimensi...  262 us
    reduce_scatter x1, waiting for transfers between devices, body(): lax.psum_scatter(grad_wup.astype(jnp.bfloat16), 'inner', scatter_dimensio...  175 us
    reduce_scatter x1, waiting for transfers between devices, body(): lax.psum_scatter(grad_wdown.astype(jnp.bfloat16), 'inner', scatter_dimens...  174 us
    psum x1, waiting for transfers between devices, body(): lax.psum(grid_w.astype(jnp.bfloat16), ('blk', 'outer')).astype(jnp.float32)  146 us
    reduce_scatter x1, waiting for transfers between devices, body(): lax.psum_scatter(grad_ptwo.astype(jnp.bfloat16), 'inner', scatter_dimensi...  144 us
    reduce_scatter x1, waiting for transfers between devices, body(): lax.psum_scatter(grad_wqkv.astype(jnp.bfloat16), 'inner', scatter_dimensi...  138 us
    all_gather x1, waiting for transfers between devices, body(): lax.all_gather(p_down, ('inner', 'outer'), axis=0, tiled=True)  123 us
    all_gather x1, waiting for transfers between devices, body(): lax.all_gather(p_up, ('inner', 'outer'), axis=0, tiled=True)  122 us
  transfers between devices with their start and end apart: 33, of which 22 were waited for; matrix products, arithmetic and copies ran while one was open for 15% of the time, Pallas kernels for 0%

profile of v1, /device:TPU:0, one launch (start us, length us, event | category | flops | bytes accessed | tf_op | source)
XLA Modules:
  0.0 2363.0 jit_solution(14549687188031615623)
XLA Ops:
  46.6 79.4 %all-reduce = bf16[20992]{0:T(1024)(128)(2,1)} all-reduce(bf16[20992]{0:T(1024)(128)(2,1)S(1)} %dynamic-update-slice), channel_id=1, replica_groups=mesh['blk'=2,'inner'=4,'outer'=4] {'inner','outer'}, use_global_device_ids=true, to_apply=%add | all-reduce | flops 20992 | bytes 83968
  162.3 10.7 collective-permute-done.3
  181.0 13.7 collective-permute-done.5
  206.3 10.9 collective-permute-done.7
  224.3 12.4 collective-permute-done.9
  243.5 14.4 all-gather.8.cloned.1.call-done
  265.8 109.3 %all-gather.10.cloned.1.call-done = bf16[1152,3456]{1,0:T(8,128)(2,1)} async-done(((bf16[72,3456]{1,0:T(8,128)(2,1)}), bf16[1152,3456]{1,0:T(8,128)(2,1)}) %all-gather.10.cloned.1.call-update) | async-done | bytes 7962640 | tf_op jit(solution)/shard_map/all_gather | solution.py:206
  404.8 12.5 collective-permute-done.15
  460.6 121.9 %all-gather.14.cloned.1.call-done = bf16[1152,4608]{1,0:T(8,128)(2,1)} async-done(((bf16[72,4608]{1,0:T(8,128)(2,1)}), bf16[1152,4608]{1,0:T(8,128)(2,1)}) %all-gather.14.cloned.1.call-update) | async-done | bytes 10616848 | tf_op jit(solution)/shard_map/all_gather | solution.py:208
  582.5 12.3 fusion.9
  594.8 122.6 %all-gather.16.cloned.1.call-done = bf16[4608,1152]{1,0:T(8,128)(2,1)} async-done(((bf16[288,1152]{1,0:T(8,128)(2,1)}), bf16[4608,1152]{1,0:T(8,128)(2,1)}) %all-gather.16.cloned.1.call-update) | async-done | bytes 10616848 | tf_op jit(solution)/shard_map/all_gather | solution.py:209
  717.4 14.5 add_convert_fusion.1
  739.1 92.0 %all-gather.18.cloned.1.call-done = bf16[2048,2048]{1,0:T(8,128)(2,1)} async-done(((bf16[128,2048]{1,0:T(8,128)(2,1)}), bf16[2048,2048]{1,0:T(8,128)(2,1)}) %all-gather.18.cloned.1.call-update) | async-done | bytes 8388624 | tf_op jit(solution)/shard_map/all_gather | solution.py:212
  831.1 11.3 fusion.20
  842.4 57.9 %all-gather.20.cloned.1.call-done = bf16[2048,768]{1,0:T(8,128)(2,1)} async-done(((bf16[128,768]{1,0:T(8,128)(2,1)}), bf16[2048,768]{1,0:T(8,128)(2,1)}) %all-gather.20.cloned.1.call-update) | async-done | bytes 3145744 | tf_op jit(solution)/shard_map/all_gather | solution.py:213
  927.9 17.5 fusion.114
  945.4 12.2 multiply_reduce_fusion.7
  978.6 10.9 bitcast_convert_fusion
  1059.0 11.1 fusion
  1070.2 13.2 fusion.1
  1117.2 49.9 %reduce-scatter.19.cloned.1.call-done = bf16[288,2048]{1,0:T(8,128)(2,1)} async-done(((bf16[1152,2048]{1,0:T(8,128)(2,1)}), bf16[288,2048]{1,0:T(8,128)(2,1)}) %reduce-scatter.19.cloned.1.call-update) | async-done | bytes 1179664 | tf_op jit(solution)/shard_map/reduce_scatter | solution.py:343
  1170.4 144.2 %reduce-scatter.21.cloned.1.call-done = bf16[512,2048]{1,0:T(8,128)(2,1)} async-done(((bf16[2048,2048]{1,0:T(8,128)(2,1)}), bf16[512,2048]{1,0:T(8,128)(2,1)}) %reduce-scatter.21.cloned.1.call-update) | async-done | bytes 2097168 | tf_op jit(solution)/shard_map/reduce_scatter | solution.py:346
  1317.8 138.4 %reduce-scatter.9.cloned.1.call-done = bf16[288,3456]{1,0:T(8,128)(2,1)} async-done(((bf16[1152,3456]{1,0:T(8,128)(2,1)}), bf16[288,3456]{1,0:T(8,128)(2,1)}) %reduce-scatter.9.cloned.1.call-update) | async-done | bytes 1990672 | tf_op jit(solution)/shard_map/reduce_scatter | solution.py:328
  1464.1 175.3 %reduce-scatter.13.cloned.1.call-done = bf16[288,4608]{1,0:T(8,128)(2,1)} async-done(((bf16[1152,4608]{1,0:T(8,128)(2,1)}), bf16[288,4608]{1,0:T(8,128)(2,1)}) %reduce-scatter.13.cloned.1.call-update) | async-done | bytes 2654224 | tf_op jit(solution)/shard_map/reduce_scatter | solution.py:334
  1649.2 173.6 %reduce-scatter.15.cloned.1.call-done = bf16[1152,1152]{1,0:T(8,128)(2,1)} async-done(((bf16[4608,1152]{1,0:T(8,128)(2,1)}), bf16[1152,1152]{1,0:T(8,128)(2,1)}) %reduce-scatter.15.cloned.1.call-update) | async-done | bytes 2654224 | tf_op jit(solution)/shard_map/reduce_scatter | solution.py:337
  1831.6 262.1 %reduce-scatter.17.cloned.1.call-done = bf16[288,6912]{1,0:T(8,128)(2,1)} async-done(((bf16[1152,6912]{1,0:T(8,128)(2,1)}), bf16[288,6912]{1,0:T(8,128)(2,1)}) %reduce-scatter.17.cloned.1.call-update) | async-done | bytes 3981328 | tf_op jit(solution)/shard_map/reduce_scatter | solution.py:340
  2115.4 18.8 all-reduce.1
  2134.4 29.0 %psum.23 = bf16[4,1312]{1,0:T(4,128)(2,1)S(1)} all-reduce(bf16[4,1312]{1,0:T(4,128)(2,1)S(1)} %convert_element_type.227), channel_id=1, replica_groups=mesh['blk'=2,'inner'=4,'outer'=4] {'blk','outer'}, use_global_device_ids=true, to_apply=%region_42.43 | all-reduce | flops 5248 | bytes 20992 | tf_op jit(solution)/shard_map/psum | solution.py:359
  2164.6 10.7 fusion.92
  2175.3 146.3 %all-reduce.4.cloned.1.call-done = bf16[4,2000896]{1,0:T(4,128)(2,1)} async-done(((bf16[4,2000896]{1,0:T(4,128)(2,1)}), bf16[4,2000896]{1,0:T(4,128)(2,1)}) %all-reduce.4.cloned.1.call-update) | async-done | bytes 16007184 | tf_op jit(solution)/shard_map/psum | solution.py:358
  2321.6 9.6 dynamic-slice_convert_fusion
  2331.2 20.1 add_multiply_fusion
  (421 shorter events, 407.7 us)
Async XLA Ops:
  7.2 250.8 %all-gather.8.cloned.1.call-start = ((), (), s32[]{:S(2)}) async-start(), calls=%async_computation.8 | async-start | bytes 16920576 | tf_op jit(solution)/shard_map/all_gather | solution.py:210
  17.0 358.1 %all-gather.10.cloned.1.call-start = ((), (), s32[]{:S(2)}) async-start(), calls=%async_computation.9 | async-start | bytes 8460288 | tf_op jit(solution)/shard_map/all_gather | solution.py:206
  18.4 434.8 %all-gather.12.cloned.1.call-start = ((), (), s32[]{:S(2)}) async-start(), calls=%async_computation.10 | async-start | bytes 2820096 | tf_op jit(solution)/shard_map/all_gather | solution.py:207
  19.3 563.2 %all-gather.14.cloned.1.call-start = ((), (), s32[]{:S(2)}) async-start(), calls=%async_computation.11 | async-start | bytes 11280384 | tf_op jit(solution)/shard_map/all_gather | solution.py:208
  24.2 693.2 %all-gather.16.cloned.1.call-start = ((), (), s32[]{:S(2)}) async-start(), calls=%async_computation.12 | async-start | bytes 11280384 | tf_op jit(solution)/shard_map/all_gather | solution.py:209
  25.9 805.2 %all-gather.18.cloned.1.call-start = ((), (), s32[]{:S(2)}) async-start(), calls=%async_computation.13 | async-start | bytes 8912896 | tf_op jit(solution)/shard_map/all_gather | solution.py:212
  30.1 870.2 %all-gather.20.cloned.1.call-start = ((), (), s32[]{:S(2)}) async-start(), calls=%async_computation.14 | async-start | bytes 3342336 | tf_op jit(solution)/shard_map/all_gather | solution.py:213
  33.6 119.7 %collective-permute-start.1 = (bf16[72,2048]{1,0:T(8,128)(2,1)}, bf16[72,2048]{1,0:T(8,128)(2,1)}, u32[]{:S(2)}, u32[]{:S(2)}) collective-permute-start(bf16[72,2048]{1,0:T(8,128)(2,1)} %slice.163), channel_id=1, source_target_pairs={{0,1},{1,2},{2,3},{3,4},{4,5},{5,6},{6,7},{7,8},{8,9},{9,10},{10,1... | collective-permute-start | bytes 884744 | tf_op jit(solution)/shard_map/ppermute | solution.py:26
  36.6 116.7 %collective-permute-start.2 = (bf16[72,2048]{1,0:T(8,128)(2,1)}, bf16[72,2048]{1,0:T(8,128)(2,1)}, u32[]{:S(2)}, u32[]{:S(2)}) collective-permute-start(bf16[72,2048]{1,0:T(8,128)(2,1)} %slice.163), channel_id=1, source_target_pairs={{0,15},{1,0},{2,1},{3,2},{4,3},{5,4},{6,5},{7,6},{8,7},{9,8},{10,9... | collective-permute-start | bytes 884744 | tf_op jit(solution)/shard_map/ppermute | solution.py:29
  44.1 1068.2 %reduce-scatter.11.cloned.1.call-start = ((), (), s32[]{:S(2)}) async-start(), calls=%async_computation.16 | async-start | bytes 3317760 | tf_op jit(solution)/shard_map/reduce_scatter | solution.py:331
  153.3 19.7 collective-permute-start.3
  153.3 26.2 %collective-permute-start.4 = (bf16[72,2048]{1,0:T(8,128)(2,1)}, bf16[72,2048]{1,0:T(8,128)(2,1)S(1)}, u32[]{:S(2)}, u32[]{:S(2)}) collective-permute-start(bf16[72,2048]{1,0:T(8,128)(2,1)} %collective-permute-done.2), channel_id=1, source_target_pairs={{0,15},{1,0},{2,1},{3,2},{4,3},{5,4},{6,5},{7,6},{8,7},{9,8},{10,9... | collective-permute-start | bytes 884744 | tf_op jit(solution)/shard_map/ppermute | solution.py:29
  173.1 21.7 collective-permute-start.5
  179.5 25.3 %collective-permute-start.6 = (bf16[72,2048]{1,0:T(8,128)(2,1)S(1)}, bf16[72,2048]{1,0:T(8,128)(2,1)S(1)}, u32[]{:S(2)}, u32[]{:S(2)}) collective-permute-start(bf16[72,2048]{1,0:T(8,128)(2,1)S(1)} %collective-permute-done.4), channel_id=1, source_target_pairs={{0,15},{1,0},{2,1},{3,2},{4,3},{5,4},{6,5},{7,6},{8,7},{9,8},{10,9... | collective-permute-start | bytes 884744 | tf_op jit(solution)/shard_map/ppermute | solution.py:29
  194.8 22.5 collective-permute-start.7
  204.8 16.7 collective-permute-start.8
  217.2 19.5 collective-permute-start.9
  236.7 149.5 %collective-permute-start.11 = (bf16[72,2048]{1,0:T(8,128)(2,1)S(1)}, bf16[72,2048]{1,0:T(8,128)(2,1)S(1)}, u32[]{:S(2)}, u32[]{:S(2)}) collective-permute-start(bf16[72,2048]{1,0:T(8,128)(2,1)S(1)} %collective-permute-done.9), channel_id=1, source_target_pairs={{0,1},{1,2},{2,3},{3,4},{4,5},{5,6},{6,7},{7,8},{8,9},{9,10},{10,1... | collective-permute-start | bytes 884744 | tf_op jit(solution)/shard_map/ppermute | solution.py:26
  236.7 150.9 %collective-permute-start.12 = (bf16[72,2048]{1,0:T(8,128)(2,1)S(1)}, bf16[72,2048]{1,0:T(8,128)(2,1)S(1)}, u32[]{:S(2)}, u32[]{:S(2)}) collective-permute-start(bf16[72,2048]{1,0:T(8,128)(2,1)S(1)} %collective-permute-done.10), channel_id=1, source_target_pairs={{0,15},{1,0},{2,1},{3,2},{4,3},{5,4},{6,5},{7,6},{8,7},{9,8},{10,9... | collective-permute-start | bytes 884744 | tf_op jit(solution)/shard_map/ppermute | solution.py:29
  385.4 46.0 %collective-permute-start = (bf16[4,128,2304]{2,1,0:T(8,128)(2,1)}, bf16[4,128,2304]{2,1,0:T(8,128)(2,1)}, u32[]{:S(2)}, u32[]{:S(2)}) collective-permute-start(bf16[4,128,2304]{2,1,0:T(8,128)(2,1)} %slice.185), channel_id=1, source_target_pairs={{16,0},{0,16},{17,1},{1,17},{18,2},{2,18},{19,3},{3,19},{20,4},{4,... | collective-permute-start | bytes 7077896 | tf_op jit(solution)/shard_map/ppermute | solution.py:39
  386.2 15.3 collective-permute-start.13
  387.6 16.5 collective-permute-start.14
  401.5 15.9 collective-permute-start.15
  965.0 149.6 %reduce-scatter.23.cloned.1.call-start = ((), (), s32[]{:S(2)}) async-start(), calls=%async_computation.22 | async-start | bytes 3932160 | tf_op jit(solution)/shard_map/reduce_scatter | solution.py:349
  970.9 196.3 %reduce-scatter.19.cloned.1.call-start = ((), (), s32[]{:S(2)}) async-start(), calls=%async_computation.20 | async-start | bytes 5898240 | tf_op jit(solution)/shard_map/reduce_scatter | solution.py:343
  978.6 336.0 %reduce-scatter.21.cloned.1.call-start = ((), (), s32[]{:S(2)}) async-start(), calls=%async_computation.21 | async-start | bytes 10485760 | tf_op jit(solution)/shard_map/reduce_scatter | solution.py:346
  989.6 466.6 %reduce-scatter.9.cloned.1.call-start = ((), (), s32[]{:S(2)}) async-start(), calls=%async_computation.15 | async-start | bytes 9953280 | tf_op jit(solution)/shard_map/reduce_scatter | solution.py:328
  1023.3 22.5 collective-permute-start.16
  1058.3 581.2 %reduce-scatter.13.cloned.1.call-start = ((), (), s32[]{:S(2)}) async-start(), calls=%async_computation.17 | async-start | bytes 13271040 | tf_op jit(solution)/shard_map/reduce_scatter | solution.py:334
  1070.1 752.7 %reduce-scatter.15.cloned.1.call-start = ((), (), s32[]{:S(2)}) async-start(), calls=%async_computation.18 | async-start | bytes 13271040 | tf_op jit(solution)/shard_map/reduce_scatter | solution.py:337
  1083.4 1010.3 %reduce-scatter.17.cloned.1.call-start = ((), (), s32[]{:S(2)}) async-start(), calls=%async_computation.19 | async-start | bytes 19906560 | tf_op jit(solution)/shard_map/reduce_scatter | solution.py:340
  1112.2 1209.4 %all-reduce.4.cloned.1.call-start = ((), (), s32[]{:S(2)}) async-start(), calls=%async_computation.23 | async-start | bytes 32014336 | tf_op jit(solution)/shard_map/psum | solution.py:358
  (94 other events, 3568.7 us)
Sparse Core Ops, SparseCore 0:
  17.1 240.8 all-gather.7
  261.2 113.7 all-gather.9
  377.7 69.6 all-gather.11
  450.1 132.4 all-gather.13
  585.7 131.6 all-gather.15
  720.1 111.0 all-gather.17
  833.9 66.3 all-gather.19
  965.1 51.1 reduce-scatter.10
  1019.1 59.9 reduce-scatter.22
  1081.9 85.2 reduce-scatter.18
  1169.5 144.9 reduce-scatter.20
  1317.4 138.7 reduce-scatter.8
  1458.7 180.7 reduce-scatter.12
  1641.6 181.1 reduce-scatter.14
  1825.2 268.4 reduce-scatter.16
  2110.4 211.2 all-reduce.3
